TPU v7x, 32 devices: a whole 2x2x4 slice. The times are simulated.
32 devices in a mesh: group: 2 (over y), beam: 4 (over z), fft: 2 (over x), sub: 2 (over core).
Axes of the slice: x: 2, y: 2, z: 4, core: 2. Of those that a mesh axis runs over, the one named last changes fastest.
Arguments:
- uv_grid: float32 [8, 2, 2048, 2048], P(('group', 'beam'), None, ('fft', 'sub')), parts along dimension 0, may hold values from -6 to 6
- beam_gain: float32 [8, 512, 512], P(('group', 'beam'), ('fft', 'sub')), parts along dimension 0, may hold values from 0.1 to 1
- sub_pixel: float32 [8, 2], P(('group', 'beam')), parts along dimension 0, may hold values from 0 to 1
- intersection_tiles: int32 [8, 4], P('group'), parts along dimension 0, may hold values from 0 to 7, as said below
- tile_offsets: int32 [8, 4, 2], P(('group', 'beam')), parts along dimension 0, may hold values from 0 to 252
Outputs:
- sky: float32 [16, 256, 256], P(('group', 'beam'), ('fft', 'sub')), parts along dimension 0
There are 2 independent parts, one for each index of `group`. A program takes and returns all parts, laid end to end along the dimension named above; each array names one. Nothing has to cross between parts.
Inputs may be any that keep to these rules, and one draw needn't show every extreme that they name: `intersection_tiles`: each row names 4 distinct sky tiles; sky tile t belongs to owner t // 2, and the tiles of beam b belong to owners b - 1 to b + 2 taken modulo the number of owners, with at most 2 of them on one owner.
All inputs are finite; a program needn't handle non-finite values.
Results may differ from a plain program's by a relative error of at most 0.0037.
Values may be sent and summed in bfloat16 or wider, within the bound.
A program may use at most 64 MiB of HBM per device.

v0:
```python
import functools

import jax
import jax.numpy as jnp
import ml_dtypes
import numpy as np
from jax import lax
from jax.experimental import pallas as pl
from jax.experimental.pallas import tpu as pltpu
from jax.sharding import PartitionSpec as P

S = 256
TILE_DEV = 2
RADIX = 4
HOPS = (1, -1, 2)
MESH = pl.DeviceIdType.MESH
F32 = jnp.float32
BF16 = jnp.bfloat16


def turns(rows, cols, length):
    angle = np.mod(np.outer(rows, cols), length) * (2.0 * np.pi / length)
    return np.cos(angle), np.sin(angle)


def column_tables(length, window):
    fold = length // RADIX
    per = window // RADIX
    tables = []
    for c in range(RADIX):
        cos, sin = turns(np.arange(fold), RADIX * np.arange(per) + c - window // 2, length)
        tables.append(np.concatenate([cos, sin], axis=1))
    full = np.stack(tables).astype(np.float32)
    high = full.astype(ml_dtypes.bfloat16)
    low = (full - high.astype(np.float32)).astype(ml_dtypes.bfloat16)
    return np.stack([high, low])


def row_tables(length, window, rows):
    cos, sin = turns(np.arange(window) - window // 2, np.arange(rows), length)
    return np.stack([cos, sin]).astype(np.float32).astype(ml_dtypes.bfloat16)


def near(a):
    return (1.5 * a - 2.5) * a * a + 1.0


def far(a):
    return ((-0.5 * a + 2.5) * a - 4.0) * a + 2.0


def taps(frac):
    return far(1.0 + frac), near(frac), near(1.0 - frac), far(2.0 - frac)


def kernel(
    groups, quarter, step, shift_ref, tiles_ref, offs_ref, gain_ref, uv_ref, col_hbm, row_hbm, out_ref,
    buf, col_ref, row_ref, table, spec, gsend, grecv, psend, precv, filt, crops,
    nsend, nrecv, dsend, drecv, znsend, znrecv, zdsend, zdrecv,
    load_sems, send_sems, recv_sems,
):
    chip, core = lax.axis_index("fft"), lax.axis_index("sub")
    chips, cores = lax.axis_size("fft"), lax.axis_size("sub")
    me = chip * cores + core
    owner = lax.axis_index("beam")
    owners = lax.axis_size("beam")
    rows, length = buf.shape[1], buf.shape[2]
    fold = length // RADIX
    window = gain_ref.shape[2]
    per = window // RADIX
    wide = window // groups
    side = S // groups
    count = offs_ref.shape[2]
    chunks = rows // step
    padded = crops.shape[2]

    def load(i):
        span = pl.ds(pl.multiple_of(i * step, step), step)
        return pltpu.make_async_copy(uv_ref.at[0, :, span], buf.at[:, span], load_sems.at[i])

    col_load = pltpu.make_async_copy(col_hbm, col_ref, load_sems.at[chunks])
    row_load = pltpu.make_async_copy(row_hbm, row_ref, load_sems.at[chunks + 1])
    row_load.start()
    col_load.start()
    for i in range(chunks):
        load(i).start()

    def beam(hop):
        return {"beam": lax.rem(owner + hop + owners, owners)}

    peers = []
    for a in list(range(1, chips)) + [0]:
        for e in range(cores):
            if a or e:
                to = (lax.rem(chip + a, chips), lax.rem(core + e, cores))
                frm = (lax.rem(chip - a + chips, chips), lax.rem(core - e + cores, cores))
                peers.append((
                    {"fft": to[0], "sub": to[1]}, to[0] * cores + to[1], frm[0] * cores + frm[1]))
    lanes = len(peers)

    barrier = pltpu.get_barrier_semaphore()
    for device, _, _ in peers:
        pl.semaphore_signal(barrier, inc=1, device_id=device, device_id_type=MESH)
    for hop in HOPS:
        pl.semaphore_signal(barrier, inc=1, device_id=beam(-hop), device_id_type=MESH)

    def remote(src, dst, index, device):
        return pltpu.make_async_remote_copy(
            src_ref=src, dst_ref=dst, send_sem=send_sems.at[index], recv_sem=recv_sems.at[index],
            device_id=device, device_id_type=MESH)

    def natural(place):
        return RADIX * jnp.bitwise_and(place, per - 1) + lax.shift_right_logical(place, per.bit_length() - 1)

    gain = gain_ref[0]
    source = lax.broadcasted_iota(jnp.int32, (window, window), 0)
    order = jnp.where(source == natural(lax.broadcasted_iota(jnp.int32, (1, window), 1)), 1.0, 0.0).astype(BF16)
    high = gain.astype(BF16)
    rest = gain - high.astype(F32)
    middle = rest.astype(BF16)
    low = (rest - middle.astype(F32)).astype(BF16)
    moved = jnp.dot(high, order, preferred_element_type=F32)
    moved += jnp.dot(middle, order, preferred_element_type=F32)
    moved += jnp.dot(low, order, preferred_element_type=F32)
    for g in range(groups):
        gsend[g] = moved[:, g * wide:(g + 1) * wide]

    pl.semaphore_wait(barrier, lanes + len(HOPS))
    gain_copies = [remote(gsend.at[to], grecv.at[me], i, device) for i, (device, to, _) in enumerate(peers)]
    for c in gain_copies:
        c.start()
    grecv[me] = gsend[me]

    row_load.wait()
    cos = row_ref[0].astype(F32)
    sin = row_ref[1].astype(F32)
    if quarter:
        turn = jnp.bitwise_and(me * lax.broadcasted_iota(jnp.int32, (window, 1), 0), 3)
        plus = jnp.where(turn == 0, 1.0, jnp.where(turn == 2, -1.0, 0.0))
        cross = jnp.where(turn == 1, 1.0, jnp.where(turn == 3, -1.0, 0.0))
        cos, sin = plus * cos - cross * sin, cross * cos + plus * sin
    table[:, :rows] = cos.astype(BF16)
    table[:, rows:] = (-sin).astype(BF16)

    down = taps(shift_ref[0, 0])
    across = taps(shift_ref[0, 1])

    def filter_rows(x):
        total = down[0] * x
        for d in range(1, 4):
            total += down[d] * pltpu.roll(x, window - d, 0)
        return total

    def filter_columns(x):
        total = across[0] * x
        for d in range(1, 4):
            total += across[d] * pltpu.roll(x, padded - d, 1)
        return total[:, :S]

    def columns(i, carry):
        load(i).wait()
        span = pl.ds(pl.multiple_of(i * step, step), step)
        a = [buf[0, span, j * fold:(j + 1) * fold] for j in range(RADIX)]
        b = [buf[1, span, j * fold:(j + 1) * fold] for j in range(RADIX)]
        ap, am, aq, an = a[0] + a[2], a[0] - a[2], a[1] + a[3], a[1] - a[3]
        bp, bm, bq, bn = b[0] + b[2], b[0] - b[2], b[1] + b[3], b[1] - b[3]
        folded = (
            (ap + aq, bp + bq),
            (am - bn, bm + an),
            (ap - aq, bp - bq),
            (am + bn, bm - an),
        )
        for c in range(RADIX):
            z = jnp.concatenate(folded[c], axis=0)
            high = z.astype(BF16)
            low = (z - high.astype(F32)).astype(BF16)
            out = jnp.dot(high, col_ref[0, c], preferred_element_type=F32)
            out += jnp.dot(low, col_ref[0, c], preferred_element_type=F32)
            out += jnp.dot(high, col_ref[1, c], preferred_element_type=F32)
            real = (out[:step, :per] - out[step:, per:]).astype(BF16)
            imag = (out[:step, per:] + out[step:, :per]).astype(BF16)
            for g in range(c * per // wide, (c + 1) * per // wide):
                at = g * wide - c * per
                spec[g, span] = real[:, at:at + wide]
                spec[g, pl.ds(pl.multiple_of(rows + i * step, step), step)] = imag[:, at:at + wide]
        return carry

    col_load.wait()
    lax.fori_loop(0, chunks // 2, columns, 0)

    for i, (device, to, frm) in enumerate(peers):
        remote(gsend.at[to], grecv.at[frm], i, device).wait_recv()
    beam_gain = grecv[...].reshape(window, wide)
    filt[1] = filter_rows(beam_gain * beam_gain)
    for k in range(count):
        top = offs_ref[0, 0, k]
        for g in range(groups):
            dsend[g, k] = filt[1, pl.ds(top + g * side, side), :]
    base = lanes
    den_copies = [
        remote(dsend.at[to], drecv.at[me], base + i, device) for i, (device, to, _) in enumerate(peers)]
    for c in den_copies:
        c.start()
    drecv[me] = dsend[me]

    lax.fori_loop(chunks // 2, chunks, columns, 0)

    base = 2 * lanes
    part_copies = []
    for i, (device, to, _) in enumerate(peers):
        share = jnp.dot(table[...], spec[to], preferred_element_type=F32) * (1.0 / length)
        psend[i] = share.astype(BF16)
        c = remote(psend.at[i], precv.at[i], base + i, device)
        c.start()
        part_copies.append(c)
    image = jnp.dot(table[...], spec[me], preferred_element_type=F32) * (1.0 / length)

    column = natural(lax.broadcasted_iota(jnp.int32, (window, 1), 0))
    target = lax.broadcasted_iota(jnp.int32, (window, padded), 1)
    for k in range(count):
        crops[k] = jnp.where(target == column - offs_ref[0, 1, k], 1.0, 0.0).astype(BF16)

    def owed(pieces, hop, slot):
        tile = lax.rem(owner + hop + owners, owners) * TILE_DEV + slot
        total = jnp.zeros((side, S), F32)
        for k in range(count):
            total += jnp.where(tiles_ref[owner, k] == tile, 1.0, 0.0) * pieces[k]
        return total

    for i, (device, to, frm) in enumerate(peers):
        remote(dsend.at[to], drecv.at[frm], lanes + i, device).wait_recv()
    pieces = []
    for k in range(count):
        den = jnp.concatenate([drecv[g, k] for g in range(groups)], axis=1)
        high = den.astype(BF16)
        low = (den - high.astype(F32)).astype(BF16)
        got = jnp.dot(jnp.concatenate([high, low], axis=0), crops[k], preferred_element_type=F32)
        pieces.append(filter_columns(got[:side] + got[side:]))
    base = 4 * lanes
    beam_copies = []
    for h, hop in enumerate(HOPS):
        for slot in range(TILE_DEV):
            zdsend[h, slot] = owed(pieces, hop, slot).astype(BF16)
        c = remote(zdsend.at[h], zdrecv.at[h], base + h, beam(hop))
        c.start()
        beam_copies.append(c)
    dens = [owed(pieces, 0, slot) for slot in range(TILE_DEV)]

    for i, c in enumerate(part_copies):
        c.wait_recv()
        image += precv[i].astype(F32)
    filt[0] = filter_rows(beam_gain * image)
    base = 3 * lanes
    num_copies = []
    for i, (device, to, _) in enumerate(peers):
        for k in range(count):
            nsend[to, k] = filt[0, pl.ds(offs_ref[0, 0, k] + to * side, side), :].astype(BF16)
        c = remote(nsend.at[to], nrecv.at[me], base + i, device)
        c.start()
        num_copies.append(c)
    for k in range(count):
        nrecv[me, k] = filt[0, pl.ds(offs_ref[0, 0, k] + me * side, side), :].astype(BF16)
    for i, (device, to, frm) in enumerate(peers):
        remote(nsend.at[to], nrecv.at[frm], base + i, device).wait_recv()

    pieces = []
    for k in range(count):
        num = jnp.concatenate([nrecv[g, k] for g in range(groups)], axis=1)
        pieces.append(filter_columns(jnp.dot(num, crops[k], preferred_element_type=F32)))
    base = 4 * lanes + len(HOPS)
    for h, hop in enumerate(HOPS):
        for slot in range(TILE_DEV):
            znsend[h, slot] = owed(pieces, hop, slot).astype(BF16)
        c = remote(znsend.at[h], znrecv.at[h], base + h, beam(hop))
        c.start()
        beam_copies.append(c)
    nums = [owed(pieces, 0, slot) for slot in range(TILE_DEV)]
    for c in beam_copies:
        c.wait_recv()
    for slot in range(TILE_DEV):
        num, den = nums[slot], dens[slot]
        for h in range(len(HOPS)):
            num += znrecv[h, slot].astype(F32)
            den += zdrecv[h, slot].astype(F32)
        out_ref[slot] = num / jnp.maximum(den, 0.5)
    for c in gain_copies + den_copies + part_copies + num_copies + beam_copies:
        c.wait_send()


def body(uv_grid, beam_gain, sub_pixel, intersection_tiles, tile_offsets):
    groups = lax.axis_size(("fft", "sub"))
    rows = uv_grid.shape[2]
    length = uv_grid.shape[3]
    own_rows = beam_gain.shape[1]
    window = beam_gain.shape[2]
    wide = window // groups
    side = S // groups
    count = tile_offsets.shape[1]
    quarter = RADIX * rows == length
    if quarter:
        row_table = jnp.asarray(row_tables(length, window, rows))
    else:
        member = lax.axis_index("fft") * lax.axis_size("sub") + lax.axis_index("sub")
        freq = member * rows + jnp.arange(rows, dtype=jnp.int32)
        place = jnp.arange(window, dtype=jnp.int32) - window // 2
        angle = jnp.mod(place[:, None] * freq[None, :], length).astype(F32) * (2.0 * np.pi / length)
        row_table = jnp.stack([jnp.cos(angle), jnp.sin(angle)]).astype(BF16)
    col_table = jnp.asarray(column_tables(length, window))
    step = min(128, rows)
    vmem = pl.BlockSpec(memory_space=pltpu.VMEM)
    smem = pl.BlockSpec(memory_space=pltpu.SMEM)
    anywhere = pl.BlockSpec(memory_space=pl.ANY)
    hops = len(HOPS)
    copies = 4 * (groups - 1) + 2 * hops
    left = (groups, count, side, wide)
    owed = (hops, TILE_DEV, side, S)
    return pl.pallas_call(
        functools.partial(kernel, groups, quarter, step),
        out_shape=jax.ShapeDtypeStruct((TILE_DEV, side, S), F32),
        in_specs=[smem, smem, smem, vmem, anywhere, anywhere, anywhere],
        out_specs=vmem,
        scratch_shapes=[
            pltpu.VMEM((2, rows, length), F32),
            pltpu.VMEM(col_table.shape, BF16),
            pltpu.VMEM(row_table.shape, BF16),
            pltpu.VMEM((window, 2 * rows), BF16),
            pltpu.VMEM((groups, 2 * rows, wide), BF16),
            pltpu.VMEM((groups, own_rows, wide), F32),
            pltpu.VMEM((groups, own_rows, wide), F32),
            pltpu.VMEM((groups - 1, window, wide), BF16),
            pltpu.VMEM((groups - 1, window, wide), BF16),
            pltpu.VMEM((2, window, wide), F32),
            pltpu.VMEM((count, window, S + 128), BF16),
            pltpu.VMEM(left, BF16),
            pltpu.VMEM(left, BF16),
            pltpu.VMEM(left, F32),
            pltpu.VMEM(left, F32),
            pltpu.VMEM(owed, BF16),
            pltpu.VMEM(owed, BF16),
            pltpu.VMEM(owed, BF16),
            pltpu.VMEM(owed, BF16),
            pltpu.SemaphoreType.DMA((rows // step + 2,)),
            pltpu.SemaphoreType.DMA((copies,)),
            pltpu.SemaphoreType.DMA((copies,)),
        ],
        compiler_params=pltpu.CompilerParams(collective_id=0, has_side_effects=True),
    )(sub_pixel, intersection_tiles, jnp.swapaxes(tile_offsets, 1, 2), beam_gain, uv_grid, col_table, row_table)


def solution(mesh):
    placed = (
        P(("group", "beam"), None, ("fft", "sub"), None),
        P(("group", "beam"), ("fft", "sub"), None),
        P(("group", "beam"), None),
        P("group", None),
        P(("group", "beam"), None, None),
    )
    return jax.shard_map(
        body,
        mesh=mesh,
        in_specs=placed,
        out_specs=P(("group", "beam"), ("fft", "sub"), None),
        check_vma=False,
    )
```

profile of v0, /device:TPU:0, one launch (start us, length us, event | category | flops | bytes accessed | tf_op | source)
XLA Modules:
  0.0 39.2 jit_solution(8894190973182173356)
XLA Ops:
  0.0 37.6 %shard_map.73 = f32[2,64,256]{2,1,0:T(8,128)} custom-call(f32[1,2]{1,0:T(1,128)} %shift_ref.1, s32[4,4]{1,0:T(4,128)} %tiles_ref.1, s32[1,2,4]{2,1,0:T(2,128)} %bitcast.1, f32[1,128,512]{2,1,0:T(8,128)} %gain_ref.1, f32[1,2,512,2048]{3,2,1,0:T(8,128)} %uv_ref.1, bf16[2,4,512,256]{3,2,1,0:T(8,128)(2,1)} %constant.5.clone.col_hbm, ...), custom_call_target="tpu_custom_call" | custom-call | tf_op jit(solution)/shard_map/pallas_call | solution.py:317
  37.6 1.6 %copy.9 = f32[2,64,256]{2,1,0:T(8,128)} copy(f32[2,64,256]{2,1,0:T(8,128)} %shard_map.73) | data formatting | bytes 262144
where the time goes:
time: 39.4 us; the launch traced here: 39.2 us
  Pallas kernels  37.6 us (95%)
  local copies, waits for them, and re-layouts  1.57 us (4%)
    pallas_call x1, Pallas kernels, body(): pl.pallas_call(functools.partial(kernel, groups, quarter, step), out_shap...  37.6 us
    unnamed x1, local copies, waits for them, and re-layouts  1.57 us

commit v1 on v0

--- a/solution.py
+++ b/solution.py
@@ -55,8 +55,8 @@
 
 def kernel(
     groups, quarter, step, shift_ref, tiles_ref, offs_ref, gain_ref, uv_ref, col_hbm, row_hbm, out_ref,
-    buf, col_ref, row_ref, table, spec, gsend, grecv, psend, precv, filt, crops,
-    nsend, nrecv, dsend, drecv, znsend, znrecv, zdsend, zdrecv,
+    buf, col_ref, row_ref, table, spec, gall, hsend, hrecv, psend, precv, filt, squares, crops,
+    nsend, nrecv, znsend, znrecv, zdsend, zdrecv,
     load_sems, send_sems, recv_sems,
 ):
     chip, core = lax.axis_index("fft"), lax.axis_index("sub")
@@ -80,10 +80,10 @@
 
     col_load = pltpu.make_async_copy(col_hbm, col_ref, load_sems.at[chunks])
     row_load = pltpu.make_async_copy(row_hbm, row_ref, load_sems.at[chunks + 1])
-    row_load.start()
     col_load.start()
     for i in range(chunks):
         load(i).start()
+    row_load.start()
 
     def beam(hop):
         return {"beam": lax.rem(owner + hop + owners, owners)}
@@ -97,6 +97,7 @@
                 peers.append((
                     {"fft": to[0], "sub": to[1]}, to[0] * cores + to[1], frm[0] * cores + frm[1]))
     lanes = len(peers)
+    shared = 2 * lanes + 1
 
     barrier = pltpu.get_barrier_semaphore()
     for device, _, _ in peers:
@@ -112,24 +113,27 @@
     def natural(place):
         return RADIX * jnp.bitwise_and(place, per - 1) + lax.shift_right_logical(place, per.bit_length() - 1)
 
-    gain = gain_ref[0]
-    source = lax.broadcasted_iota(jnp.int32, (window, window), 0)
-    order = jnp.where(source == natural(lax.broadcasted_iota(jnp.int32, (1, window), 1)), 1.0, 0.0).astype(BF16)
-    high = gain.astype(BF16)
-    rest = gain - high.astype(F32)
-    middle = rest.astype(BF16)
-    low = (rest - middle.astype(F32)).astype(BF16)
-    moved = jnp.dot(high, order, preferred_element_type=F32)
-    moved += jnp.dot(middle, order, preferred_element_type=F32)
-    moved += jnp.dot(low, order, preferred_element_type=F32)
-    for g in range(groups):
-        gsend[g] = moved[:, g * wide:(g + 1) * wide]
+    own_rows = gain_ref.shape[1]
+
+    def rows_of(member):
+        return gall.at[pl.ds(pl.multiple_of(member * own_rows, own_rows), own_rows)]
+
+    def at(a, e):
+        other = lax.rem(chip + a + chips, chips), lax.rem(core + e + cores, cores)
+        return {"fft": other[0], "sub": other[1]}, other[0] * cores + other[1]
+
+    def slot_of(a, e):
+        return a * cores + e
 
     pl.semaphore_wait(barrier, lanes + len(HOPS))
-    gain_copies = [remote(gsend.at[to], grecv.at[me], i, device) for i, (device, to, _) in enumerate(peers)]
+    gain_copies = []
+    for a in list(range(1, chips)) + [0]:
+        for e in range(cores):
+            if (a == 0) != (e == 0):
+                gain_copies.append(remote(gain_ref.at[0], rows_of(me), slot_of(a, e), at(a, e)[0]))
     for c in gain_copies:
         c.start()
-    grecv[me] = gsend[me]
+    gall[pl.ds(pl.multiple_of(me * own_rows, own_rows), own_rows), :] = gain_ref[0]
 
     row_load.wait()
     cos = row_ref[0].astype(F32)
@@ -187,33 +191,53 @@
 
     col_load.wait()
     lax.fori_loop(0, chunks // 2, columns, 0)
-
-    for i, (device, to, frm) in enumerate(peers):
-        remote(gsend.at[to], grecv.at[frm], i, device).wait_recv()
-    beam_gain = grecv[...].reshape(window, wide)
-    filt[1] = filter_rows(beam_gain * beam_gain)
-    for k in range(count):
-        top = offs_ref[0, 0, k]
-        for g in range(groups):
-            dsend[g, k] = filt[1, pl.ds(top + g * side, side), :]
-    base = lanes
-    den_copies = [
-        remote(dsend.at[to], drecv.at[me], base + i, device) for i, (device, to, _) in enumerate(peers)]
-    for c in den_copies:
-        c.start()
-    drecv[me] = dsend[me]
-
+    for a in range(1, chips):
+        remote(gain_ref.at[0], rows_of(at(-a, 0)[1]), slot_of(a, 0), at(a, 0)[0]).wait_recv()
+        for e in range(1, cores):
+            c = remote(rows_of(at(-a, 0)[1]), rows_of(at(-a, 0)[1]), slot_of(a, e), at(0, e)[0])
+            c.start()
+            gain_copies.append(c)
     lax.fori_loop(chunks // 2, chunks, columns, 0)
 
-    base = 2 * lanes
+    def share(member):
+        return jnp.dot(table[...], spec[member], preferred_element_type=F32) * (1.0 / length)
+
+    base = lanes + 1
     part_copies = []
-    for i, (device, to, _) in enumerate(peers):
-        share = jnp.dot(table[...], spec[to], preferred_element_type=F32) * (1.0 / length)
-        psend[i] = share.astype(BF16)
-        c = remote(psend.at[i], precv.at[i], base + i, device)
+    core_copies = {}
+    for e in range(1, cores):
+        for a in list(range(1, chips)) + [0]:
+            i = (e - 1) * chips + a
+            hsend[i] = share(at(a, e)[1]).astype(BF16)
+            c = remote(hsend.at[i], hrecv.at[i], base + i, at(0, e)[0])
+            c.start()
+            core_copies[a, e] = c
+    base += (cores - 1) * chips
+    for a in range(1, chips):
+        total = share(at(a, 0)[1])
+        for e in range(1, cores):
+            core_copies[a, e].wait_recv()
+            total += hrecv[(e - 1) * chips + a].astype(F32)
+        psend[a - 1] = total.astype(BF16)
+        c = remote(psend.at[a - 1], precv.at[a - 1], base + a - 1, at(a, 0)[0])
         c.start()
         part_copies.append(c)
-    image = jnp.dot(table[...], spec[me], preferred_element_type=F32) * (1.0 / length)
+    image = share(me)
+    for e in range(1, cores):
+        core_copies[0, e].wait_recv()
+        image += hrecv[(e - 1) * chips].astype(F32)
+
+    for a in range(chips):
+        for e in range(1, cores):
+            frm = at(-a, -e)[1]
+            remote(rows_of(frm), rows_of(frm), slot_of(a, e), at(0, e)[0]).wait_recv()
+    source = lax.broadcasted_iota(jnp.int32, (window, wide), 0)
+    order = jnp.where(source == natural(me * wide + lax.broadcasted_iota(jnp.int32, (1, wide), 1)), 1.0, 0.0)
+    order = order.astype(BF16)
+    gain = gall[...]
+    high = gain.astype(BF16)
+    low = (gain - high.astype(F32)).astype(BF16)
+    beam_gain = jnp.dot(high, order, preferred_element_type=F32) + jnp.dot(low, order, preferred_element_type=F32)
 
     column = natural(lax.broadcasted_iota(jnp.int32, (window, 1), 0))
     target = lax.broadcasted_iota(jnp.int32, (window, padded), 1)
@@ -227,16 +251,20 @@
             total += jnp.where(tiles_ref[owner, k] == tile, 1.0, 0.0) * pieces[k]
         return total
 
-    for i, (device, to, frm) in enumerate(peers):
-        remote(dsend.at[to], drecv.at[frm], lanes + i, device).wait_recv()
     pieces = []
+    for q in range(window // 128):
+        g = gall[:, q * 128:(q + 1) * 128]
+        squares[q] = filter_rows(g * g)
+    place = lax.broadcasted_iota(jnp.int32, (window, 1), 0)
     for k in range(count):
-        den = jnp.concatenate([drecv[g, k] for g in range(groups)], axis=1)
+        den = jnp.concatenate(
+            [squares[q, pl.ds(offs_ref[0, 0, k] + me * side, side), :] for q in range(window // 128)], axis=1)
         high = den.astype(BF16)
         low = (den - high.astype(F32)).astype(BF16)
-        got = jnp.dot(jnp.concatenate([high, low], axis=0), crops[k], preferred_element_type=F32)
+        crop = jnp.where(target == place - offs_ref[0, 1, k], 1.0, 0.0).astype(BF16)
+        got = jnp.dot(jnp.concatenate([high, low], axis=0), crop, preferred_element_type=F32)
         pieces.append(filter_columns(got[:side] + got[side:]))
-    base = 4 * lanes
+    base = shared
     beam_copies = []
     for h, hop in enumerate(HOPS):
         for slot in range(TILE_DEV):
@@ -249,17 +277,17 @@
     for i, c in enumerate(part_copies):
         c.wait_recv()
         image += precv[i].astype(F32)
-    filt[0] = filter_rows(beam_gain * image)
-    base = 3 * lanes
+    filt[...] = filter_rows(beam_gain * image)
+    base = shared + 2 * len(HOPS)
     num_copies = []
     for i, (device, to, _) in enumerate(peers):
         for k in range(count):
-            nsend[to, k] = filt[0, pl.ds(offs_ref[0, 0, k] + to * side, side), :].astype(BF16)
+            nsend[to, k] = filt[pl.ds(offs_ref[0, 0, k] + to * side, side), :].astype(BF16)
         c = remote(nsend.at[to], nrecv.at[me], base + i, device)
         c.start()
         num_copies.append(c)
     for k in range(count):
-        nrecv[me, k] = filt[0, pl.ds(offs_ref[0, 0, k] + me * side, side), :].astype(BF16)
+        nrecv[me, k] = filt[pl.ds(offs_ref[0, 0, k] + me * side, side), :].astype(BF16)
     for i, (device, to, frm) in enumerate(peers):
         remote(nsend.at[to], nrecv.at[frm], base + i, device).wait_recv()
 
@@ -267,7 +295,7 @@
     for k in range(count):
         num = jnp.concatenate([nrecv[g, k] for g in range(groups)], axis=1)
         pieces.append(filter_columns(jnp.dot(num, crops[k], preferred_element_type=F32)))
-    base = 4 * lanes + len(HOPS)
+    base = shared + len(HOPS)
     for h, hop in enumerate(HOPS):
         for slot in range(TILE_DEV):
             znsend[h, slot] = owed(pieces, hop, slot).astype(BF16)
@@ -283,7 +311,7 @@
             num += znrecv[h, slot].astype(F32)
             den += zdrecv[h, slot].astype(F32)
         out_ref[slot] = num / jnp.maximum(den, 0.5)
-    for c in gain_copies + den_copies + part_copies + num_copies + beam_copies:
+    for c in gain_copies + list(core_copies.values()) + part_copies + num_copies + beam_copies:
         c.wait_send()
 
 
@@ -311,7 +339,8 @@
     smem = pl.BlockSpec(memory_space=pltpu.SMEM)
     anywhere = pl.BlockSpec(memory_space=pl.ANY)
     hops = len(HOPS)
-    copies = 4 * (groups - 1) + 2 * hops
+    copies = 3 * (groups - 1) + 1 + 2 * hops
+    chips, cores = lax.axis_size("fft"), lax.axis_size("sub")
     left = (groups, count, side, wide)
     owed = (hops, TILE_DEV, side, S)
     return pl.pallas_call(
@@ -325,16 +354,16 @@
             pltpu.VMEM(row_table.shape, BF16),
             pltpu.VMEM((window, 2 * rows), BF16),
             pltpu.VMEM((groups, 2 * rows, wide), BF16),
-            pltpu.VMEM((groups, own_rows, wide), F32),
-            pltpu.VMEM((groups, own_rows, wide), F32),
-            pltpu.VMEM((groups - 1, window, wide), BF16),
-            pltpu.VMEM((groups - 1, window, wide), BF16),
-            pltpu.VMEM((2, window, wide), F32),
+            pltpu.VMEM((window, window), F32),
+            pltpu.VMEM(((cores - 1) * chips, window, wide), BF16),
+            pltpu.VMEM(((cores - 1) * chips, window, wide), BF16),
+            pltpu.VMEM((chips - 1, window, wide), BF16),
+            pltpu.VMEM((chips - 1, window, wide), BF16),
+            pltpu.VMEM((window, wide), F32),
+            pltpu.VMEM((window // 128, window, 128), F32),
             pltpu.VMEM((count, window, S + 128), BF16),
             pltpu.VMEM(left, BF16),
             pltpu.VMEM(left, BF16),
-            pltpu.VMEM(left, F32),
-            pltpu.VMEM(left, F32),
             pltpu.VMEM(owed, BF16),
             pltpu.VMEM(owed, BF16),
             pltpu.VMEM(owed, BF16),

time: 39.4 us -> 37.2 us (0.944)
  Pallas kernels: 37.6 us -> 35.5 us
    pallas_call x1, Pallas kernels: 37.6 us -> 35.5 us  [body(): pl.pallas_call(functools.partial(kernel, groups, quarter, step), out_shap...]
where the time goes in v1:
time: 37.2 us; the launch traced here: 37 us
  Pallas kernels  35.5 us (95%)
  local copies, waits for them, and re-layouts  1.57 us (4%)
    pallas_call x1, Pallas kernels, body(): pl.pallas_call(functools.partial(kernel, groups, quarter, step), out_shap...  35.5 us
    unnamed x1, local copies, waits for them, and re-layouts  1.57 us

profile of v1, /device:TPU:0, one launch (start us, length us, event | category | flops | bytes accessed | tf_op | source)
XLA Modules:
  0.0 37.0 jit_solution(17514000637608422507)
XLA Ops:
  0.0 35.5 %shard_map.73 = f32[2,64,256]{2,1,0:T(8,128)} custom-call(f32[1,2]{1,0:T(1,128)} %shift_ref.1, s32[4,4]{1,0:T(4,128)} %tiles_ref.1, s32[1,2,4]{2,1,0:T(2,128)} %bitcast.1, f32[1,128,512]{2,1,0:T(8,128)} %gain_ref.1, f32[1,2,512,2048]{3,2,1,0:T(8,128)} %uv_ref.1, bf16[2,4,512,256]{3,2,1,0:T(8,128)(2,1)} %constant.5.clone.col_hbm, ...), custom_call_target="tpu_custom_call" | custom-call | tf_op jit(solution)/shard_map/pallas_call | solution.py:346
  35.5 1.6 %copy.9 = f32[2,64,256]{2,1,0:T(8,128)} copy(f32[2,64,256]{2,1,0:T(8,128)} %shard_map.73) | data formatting | bytes 262144

commit v2 on v1

--- a/solution.py
+++ b/solution.py
@@ -134,17 +134,6 @@
     for c in gain_copies:
         c.start()
     gall[pl.ds(pl.multiple_of(me * own_rows, own_rows), own_rows), :] = gain_ref[0]
-
-    row_load.wait()
-    cos = row_ref[0].astype(F32)
-    sin = row_ref[1].astype(F32)
-    if quarter:
-        turn = jnp.bitwise_and(me * lax.broadcasted_iota(jnp.int32, (window, 1), 0), 3)
-        plus = jnp.where(turn == 0, 1.0, jnp.where(turn == 2, -1.0, 0.0))
-        cross = jnp.where(turn == 1, 1.0, jnp.where(turn == 3, -1.0, 0.0))
-        cos, sin = plus * cos - cross * sin, cross * cos + plus * sin
-    table[:, :rows] = cos.astype(BF16)
-    table[:, rows:] = (-sin).astype(BF16)
 
     down = taps(shift_ref[0, 0])
     across = taps(shift_ref[0, 1])
@@ -191,12 +180,16 @@
 
     col_load.wait()
     lax.fori_loop(0, chunks // 2, columns, 0)
-    for a in range(1, chips):
-        remote(gain_ref.at[0], rows_of(at(-a, 0)[1]), slot_of(a, 0), at(a, 0)[0]).wait_recv()
-        for e in range(1, cores):
-            c = remote(rows_of(at(-a, 0)[1]), rows_of(at(-a, 0)[1]), slot_of(a, e), at(0, e)[0])
-            c.start()
-            gain_copies.append(c)
+    row_load.wait()
+    cos = row_ref[0].astype(F32)
+    sin = row_ref[1].astype(F32)
+    if quarter:
+        turn = jnp.bitwise_and(me * lax.broadcasted_iota(jnp.int32, (window, 1), 0), 3)
+        plus = jnp.where(turn == 0, 1.0, jnp.where(turn == 2, -1.0, 0.0))
+        cross = jnp.where(turn == 1, 1.0, jnp.where(turn == 3, -1.0, 0.0))
+        cos, sin = plus * cos - cross * sin, cross * cos + plus * sin
+    table[:, :rows] = cos.astype(BF16)
+    table[:, rows:] = (-sin).astype(BF16)
     lax.fori_loop(chunks // 2, chunks, columns, 0)
 
     def share(member):
@@ -222,10 +215,21 @@
         c = remote(psend.at[a - 1], precv.at[a - 1], base + a - 1, at(a, 0)[0])
         c.start()
         part_copies.append(c)
+    for a in range(1, chips):
+        remote(gain_ref.at[0], rows_of(at(-a, 0)[1]), slot_of(a, 0), at(a, 0)[0]).wait_recv()
+        for e in range(1, cores):
+            c = remote(rows_of(at(-a, 0)[1]), rows_of(at(-a, 0)[1]), slot_of(a, e), at(0, e)[0])
+            c.start()
+            gain_copies.append(c)
     image = share(me)
     for e in range(1, cores):
         core_copies[0, e].wait_recv()
         image += hrecv[(e - 1) * chips].astype(F32)
+
+    column = natural(lax.broadcasted_iota(jnp.int32, (window, 1), 0))
+    target = lax.broadcasted_iota(jnp.int32, (window, padded), 1)
+    for k in range(count):
+        crops[k] = jnp.where(target == column - offs_ref[0, 1, k], 1.0, 0.0).astype(BF16)
 
     for a in range(chips):
         for e in range(1, cores):
@@ -238,11 +242,6 @@
     high = gain.astype(BF16)
     low = (gain - high.astype(F32)).astype(BF16)
     beam_gain = jnp.dot(high, order, preferred_element_type=F32) + jnp.dot(low, order, preferred_element_type=F32)
-
-    column = natural(lax.broadcasted_iota(jnp.int32, (window, 1), 0))
-    target = lax.broadcasted_iota(jnp.int32, (window, padded), 1)
-    for k in range(count):
-        crops[k] = jnp.where(target == column - offs_ref[0, 1, k], 1.0, 0.0).astype(BF16)
 
     def owed(pieces, hop, slot):
         tile = lax.rem(owner + hop + owners, owners) * TILE_DEV + slot

time: 37.2 us -> 33.1 us (0.89)
  Pallas kernels: 35.5 us -> 31.3 us
    pallas_call x1, Pallas kernels: 35.5 us -> 31.3 us  [body(): pl.pallas_call(functools.partial(kernel, groups, quarter, step), out_shap...]
where the time goes in v2:
time: 33.1 us; the launch traced here: 32.9 us
  Pallas kernels  31.3 us (95%)
  local copies, waits for them, and re-layouts  1.57 us (5%)
    pallas_call x1, Pallas kernels, body(): pl.pallas_call(functools.partial(kernel, groups, quarter, step), out_shap...  31.3 us
    unnamed x1, local copies, waits for them, and re-layouts  1.57 us

profile of v2, /device:TPU:0, one launch (start us, length us, event | category | flops | bytes accessed | tf_op | source)
XLA Modules:
  0.0 32.9 jit_solution(9062813118644731230)
XLA Ops:
  0.0 31.3 %shard_map.73 = f32[2,64,256]{2,1,0:T(8,128)} custom-call(f32[1,2]{1,0:T(1,128)} %shift_ref.1, s32[4,4]{1,0:T(4,128)} %tiles_ref.1, s32[1,2,4]{2,1,0:T(2,128)} %bitcast.1, f32[1,128,512]{2,1,0:T(8,128)} %gain_ref.1, f32[1,2,512,2048]{3,2,1,0:T(8,128)} %uv_ref.1, bf16[2,4,512,256]{3,2,1,0:T(8,128)(2,1)} %constant.5.clone.col_hbm, ...), custom_call_target="tpu_custom_call" | custom-call | tf_op jit(solution)/shard_map/pallas_call | solution.py:345
  31.3 1.6 %copy.9 = f32[2,64,256]{2,1,0:T(8,128)} copy(f32[2,64,256]{2,1,0:T(8,128)} %shard_map.73) | data formatting | bytes 262144
